TPU v7x, 256 devices: a whole 4x4x8 slice. The times are simulated.
256 devices in a mesh: pages: 32 (over x, y, core), mlp: 8 (over z).
Axes of the slice: x: 4, y: 4, z: 8, core: 2. Of those that a mesh axis runs over, the one named last changes fastest.
Arguments:
- embeddings: bfloat16 [8192, 1024], P('pages', 'mlp'), may hold values from -6 to 6
- w_query: bfloat16 [1024, 1024], P(None, 'mlp'), may hold values from -0.1875 to 0.1875
- w_key: bfloat16 [1024, 1024], P(None, 'mlp'), may hold values from -0.1875 to 0.1875
- w_value: bfloat16 [1024, 1024], P(None, 'mlp'), may hold values from -0.1875 to 0.1875
- w_global_query: bfloat16 [1024, 1024], P(None, 'mlp'), may hold values from -0.1875 to 0.1875
- w_out: bfloat16 [1024, 1024], P('mlp'), may hold values from -0.75 to 0.75
- w_up: bfloat16 [1024, 4096], P(None, 'mlp'), may hold values from -0.1875 to 0.1875
- w_down: bfloat16 [4096, 1024], P('mlp'), may hold values from -0.09375 to 0.09375
- norm1_gain: float32 [1024], replicated, may hold values from 0.1 to 1.9
- norm1_bias: float32 [1024], replicated, may hold values from -3 to 3
- norm2_gain: float32 [1024], replicated, may hold values from 0.1 to 1.9
- norm2_bias: float32 [1024], replicated, may hold values from -3 to 3
- cache_keys: bfloat16 [2048, 128, 1024], P('pages', None, 'mlp'), may hold values from -48 to 48
- cache_values: bfloat16 [2048, 128, 1024], P('pages', None, 'mlp'), may hold values from -6 to 6
- lengths: int32 [32], replicated, may hold values from 1 to 8192, as said below
- page_table: int32 [32, 64], replicated, may hold values from -1 to 2047, as said below
- accept: int32 [2, 8192], P(None, 'pages'), may hold values 0 or 1
Outputs:
- refined: bfloat16 [8192, 1024], P('pages', 'mlp')
Inputs may be any that keep to these rules, and one draw needn't show every extreme that they name: `lengths`: one request has exactly 8192 cached tokens. page_table[r, j] is the global slot (holder index times 64 plus local slot) of page j of request r for j < ceil(lengths[r] / 128), and -1 for later j; no slot is named twice; the pages of one request lie on at most 8 page holders, at most 8 on one holder, and the longest request has exactly 8 on each of 8 holders.
All inputs are finite; a program needn't handle non-finite values. No bound on the sum of `accept` on one device may be relied on, other than what follows from the above.
Results may differ from a plain program's by a relative error of at most 0.01.
The roundings to bfloat16 on the way count: a program that leaves them out, or rounds other values in their place, can miss the bound.
Values may be sent and summed in bfloat16 or wider, within the bound.
No kernel may reach another device: no remote copies, remote signals or barrier semaphores. Data moves between devices by JAX's collectives and lax.ppermute only.
A program may use at most 128 MiB of HBM per device.

v0:
```python
import jax
import jax.numpy as jnp
from jax import lax
from jax.sharding import PartitionSpec as P

D = 1024
HD = 64
BLK = 256


neg_big = -1e30
eps_norm = 1e-05
group_size = 8


def scaled(values_in, factor):
    head_count = factor.shape[-2]
    shape_in = values_in.shape
    split_heads = values_in.reshape(shape_in[:-1] + (head_count, shape_in[-1] // head_count))
    return (split_heads * jnp.swapaxes(factor, -1, -2)[..., None]).reshape(shape_in)


def page_scores(queries, page_keys, page_values, usable):
    scores = jnp.einsum(
        "sqhd,skhd->shqk", queries, page_keys, preferred_element_type=jnp.float32
    ) * HD ** (-0.5)
    masking = usable[:, None, None, :]
    row_peak = jnp.max(jnp.where(masking, scores, neg_big), axis=-1)
    weights = jnp.where(masking, jnp.exp(scores - row_peak[..., None]), 0.0)
    totals = jnp.sum(weights, axis=-1)
    weighted = jnp.einsum(
        "shqk,skhd->sqhd",
        weights.astype(jnp.bfloat16),
        page_values,
        preferred_element_type=jnp.float32,
    )
    return (weighted.reshape(weighted.shape[0], weighted.shape[1], -1), row_peak, totals)


def attend_pages(
    queries, page_keys, page_values, owners, page_of, limits, visit_order, visit_count
):
    request_count, block_rows, head_width = queries.shape
    head_count = head_width // HD
    page_rows = page_keys.shape[1]
    initial = (
        jnp.zeros((request_count, block_rows, head_width), jnp.float32),
        jnp.full((request_count, head_count, block_rows), neg_big, jnp.float32),
        jnp.zeros((request_count, head_count, block_rows), jnp.float32),
    )

    def one_turn(turn_index, state_now):
        run_weighted, run_peak, run_total = state_now
        chosen = lax.dynamic_slice_in_dim(visit_order, turn_index * group_size, group_size)
        holders_of = owners[chosen]
        occupied = holders_of >= 0
        safe_index = jnp.maximum(holders_of, 0)
        target = jnp.where(occupied, holders_of, request_count)
        group_keys = page_keys[chosen].reshape(group_size, page_rows, head_count, HD)
        group_values = page_values[chosen].reshape(group_size, page_rows, head_count, HD)
        group_queries = queries[safe_index].reshape(group_size, block_rows, head_count, HD)
        position = (
            page_of[chosen][:, None] * page_rows + jnp.arange(page_rows, dtype=jnp.int32)[None, :]
        )
        usable = occupied[:, None] & (position < limits[safe_index][:, None])
        weighted, row_peak, totals = page_scores(group_queries, group_keys, group_values, usable)
        sharing = (holders_of[:, None] == holders_of[None, :]) & occupied[:, None]
        group_peak = jnp.max(jnp.where(sharing[:, :, None, None], row_peak[None], neg_big), axis=1)
        old_peak = run_peak[safe_index]
        new_peak = jnp.maximum(old_peak, group_peak)
        keep_factor = jnp.exp(old_peak - new_peak)
        add_factor = jnp.where(occupied[:, None, None], jnp.exp(row_peak - new_peak), 0.0)
        sharing_float = sharing.astype(jnp.float32)
        add_total = jnp.einsum(
            "ts,shq->thq", sharing_float, totals * add_factor, precision=lax.Precision.HIGHEST
        )
        add_weighted = jnp.einsum(
            "ts,sqw->tqw",
            sharing_float,
            scaled(weighted, add_factor),
            precision=lax.Precision.HIGHEST,
        )
        new_total = run_total[safe_index] * keep_factor + add_total
        new_weighted = scaled(run_weighted[safe_index], keep_factor) + add_weighted
        return (
            run_weighted.at[target].set(new_weighted, mode="drop"),
            run_peak.at[target].set(new_peak, mode="drop"),
            run_total.at[target].set(new_total, mode="drop"),
        )

    turn_total = (visit_count + group_size - 1) // group_size
    return lax.fori_loop(0, turn_total, one_turn, initial)


def slot_owners(page_table, first_slot, slot_count):
    slot_ids = first_slot + jnp.arange(slot_count, dtype=jnp.int32)
    matches = (page_table[:, :, None] == slot_ids[None, None, :]).astype(jnp.int32)
    request_ids = jnp.arange(page_table.shape[0], dtype=jnp.int32)[:, None, None]
    page_ids = jnp.arange(page_table.shape[1], dtype=jnp.int32)[None, :, None]
    occupied = jnp.sum(matches, axis=(0, 1)) > 0
    owners = jnp.where(occupied, jnp.sum(matches * request_ids, axis=(0, 1)), -1)
    return (owners, jnp.sum(matches * page_ids, axis=(0, 1)))


def compact(occupied):
    slot_total = occupied.shape[0]
    sort_keys = jnp.where(occupied, 0, slot_total) + jnp.arange(slot_total, dtype=jnp.int32)
    return (jnp.argsort(sort_keys), jnp.sum(occupied.astype(jnp.int32)))


def finish(partials, block_part):
    part_weighted, part_peak, part_total = partials
    block_weighted, block_peak, block_total = block_part
    row_peak = jnp.maximum(block_peak, jnp.max(part_peak, axis=0))
    part_factor = jnp.exp(part_peak - row_peak[None])
    block_factor = jnp.exp(block_peak - row_peak)
    denominator = block_total * block_factor + jnp.sum(part_total * part_factor, axis=0)
    numerator = scaled(block_weighted, block_factor) + jnp.sum(
        scaled(part_weighted, part_factor), axis=0
    )
    return scaled(numerator, 1.0 / denominator).astype(jnp.bfloat16)


def norm_shares(totals, gain, bias):
    sums_pair = lax.psum((jnp.sum(totals, axis=1), jnp.sum(totals * totals, axis=1)), "mlp")
    row_mean = sums_pair[0][:, None] / D
    square = sums_pair[1][:, None] / D
    inverse = lax.rsqrt(square - row_mean * row_mean + eps_norm)
    return ((totals - row_mean) * inverse * gain + bias).astype(jnp.bfloat16)


def gather_features(shares):
    return lax.all_gather(shares, "mlp", axis=1, tiled=True)


def per_device(
    embeddings,
    w_query,
    w_key,
    w_value,
    w_global_query,
    w_out,
    w_up,
    w_down,
    norm1_gain,
    norm1_bias,
    norm2_gain,
    norm2_bias,
    cache_keys,
    cache_values,
    lengths,
    page_table,
    accept,
):
    page_count = lax.axis_size("pages")
    holder_index = lax.axis_index("pages")
    shard_index = lax.axis_index("mlp")
    row_count, own_width = embeddings.shape
    request_count = lengths.shape[0]
    per_holder = request_count // page_count
    head_width = w_query.shape[1]
    head_count = head_width // HD
    slot_count = cache_keys.shape[0]
    owners, page_of = slot_owners(page_table, holder_index * slot_count, slot_count)
    visit_order, visit_count = compact(owners >= 0)
    x_own = embeddings
    x_full = gather_features(embeddings)
    for pass_index in range(2):
        queries = jnp.dot(x_full, w_query, preferred_element_type=jnp.float32).astype(jnp.bfloat16)
        key_rows = jnp.dot(x_full, w_key, preferred_element_type=jnp.float32).astype(jnp.bfloat16)
        value_rows = jnp.dot(x_full, w_value, preferred_element_type=jnp.float32).astype(
            jnp.bfloat16
        )
        global_rows = jnp.dot(x_full, w_global_query, preferred_element_type=jnp.float32).astype(
            jnp.bfloat16
        )
        block_shape = (per_holder, BLK, head_count, HD)
        block_part = page_scores(
            queries.reshape(block_shape),
            key_rows.reshape(block_shape),
            value_rows.reshape(block_shape),
            jnp.ones((per_holder, BLK), jnp.bool_),
        )
        everyone = lax.all_gather(global_rows, "pages", axis=0, tiled=True).reshape(
            request_count, BLK, head_width
        )
        gathered = attend_pages(
            everyone, cache_keys, cache_values, owners, page_of, lengths, visit_order, visit_count
        )
        returned = (
            lax.all_to_all(gathered[0], "pages", split_axis=0, concat_axis=0, tiled=True),
            lax.all_to_all(gathered[1], "pages", split_axis=0, concat_axis=0, tiled=True),
            lax.all_to_all(gathered[2], "pages", split_axis=0, concat_axis=0, tiled=True),
        )
        partials = (
            returned[0].reshape(page_count, per_holder, BLK, head_width),
            returned[1].reshape(page_count, per_holder, head_count, BLK),
            returned[2].reshape(page_count, per_holder, head_count, BLK),
        )
        attention = finish(partials, block_part).reshape(row_count, head_width)
        attn_term = jnp.dot(attention, w_out, preferred_element_type=jnp.float32)
        accepted = accept[pass_index][:, None] != 0
        column_start = shard_index * own_width
        gain_first = lax.dynamic_slice_in_dim(norm1_gain, column_start, own_width)
        bias_first = lax.dynamic_slice_in_dim(norm1_bias, column_start, own_width)
        gain_second = lax.dynamic_slice_in_dim(norm2_gain, column_start, own_width)
        bias_second = lax.dynamic_slice_in_dim(norm2_bias, column_start, own_width)
        attn_own = lax.psum_scatter(attn_term, "mlp", scatter_dimension=1, tiled=True)
        hidden_own = norm_shares(x_own.astype(jnp.float32) + attn_own, gain_first, bias_first)
        up_proj = jnp.dot(
            lax.all_gather(hidden_own, "mlp", axis=1, tiled=True),
            w_up,
            preferred_element_type=jnp.float32,
        )
        active = jax.nn.gelu(up_proj, approximate=False).astype(jnp.bfloat16)
        down_own = lax.psum_scatter(
            jnp.dot(active, w_down, preferred_element_type=jnp.float32),
            "mlp",
            scatter_dimension=1,
            tiled=True,
        )
        layer_out = norm_shares(hidden_own.astype(jnp.float32) + down_own, gain_second, bias_second)
        x_own = jnp.where(accepted, layer_out, x_own)
        if pass_index == 0:
            x_full = gather_features(x_own)
    return x_own


def solution(mesh):
    return jax.shard_map(
        per_device,
        mesh=mesh,
        in_specs=(
            P("pages", "mlp"),
            P(None, "mlp"),
            P(None, "mlp"),
            P(None, "mlp"),
            P(None, "mlp"),
            P("mlp", None),
            P(None, "mlp"),
            P("mlp", None),
            P(),
            P(),
            P(),
            P(),
            P("pages", None, "mlp"),
            P("pages", None, "mlp"),
            P(),
            P(),
            P(None, "pages"),
        ),
        out_specs=P("pages", "mlp"),
        check_vma=False,
    )
```

profile of v0, /device:TPU:9, one launch (start us, length us, event | category | flops | bytes accessed | tf_op | source)
XLA Modules:
  0.0 990.0 jit_solution(3612409518881204513)
XLA Ops:
  6.5 23.5 %all_gather.18 = bf16[256,1024]{1,0:T(8,128)(2,1)S(1)} all-gather(bf16[256,128]{1,0:T(8,128)(2,1)} %param.21), channel_id=1, replica_groups=mesh['pages'=32,'mlp'=8] {'mlp'}, dimensions={1}, use_global_device_ids=true | all-gather | bytes 589824 | tf_op jit(solution)/shard_map/all_gather | solution.py:133
  37.5 47.2 %all-gather.3.cloned.1.call-done = bf16[8192,128]{1,0:T(8,128)(2,1)} async-done(((bf16[256,128]{1,0:T(8,128)(2,1)}), bf16[8192,128]{1,0:T(8,128)(2,1)}) %all-gather.3.cloned.1.call-update) | async-done | bytes 2097168 | tf_op jit(solution)/shard_map/all_gather | solution.py:184
  87.7 155.2 %while.28 = (s32[]{:T(128)}, f32[32,256,128]{2,1,0:T(8,128)}, f32[32,2,256]{2,1,0:T(2,128)}, f32[32,2,256]{2,1,0:T(2,128)S(1)}, s32[]{:T(128)}, /*index=5*/s32[6...) while((s32[]{:T(128)}, f32[32,256,128]{2,1,0:T(8,128)}, ...), condition=%wide.region_13.14_spmd, body=%wide.region_6.13_spmd.sunk | while | flops 166442464 | bytes 29996440 | solution.py:92
  99.2 2.8 gather_fusion.7
  110.8 2.5 copy.305
  113.3 2.5 convolution_add_fusion.8
  116.0 2.8 scatter_fusion
  130.2 2.8 gather_fusion.7
  141.8 2.5 copy.305
  144.4 2.5 convolution_add_fusion.8
  147.0 2.8 scatter_fusion
  161.3 2.8 gather_fusion.7
  172.9 2.5 copy.305
  175.4 2.5 convolution_add_fusion.8
  178.1 2.8 scatter_fusion
  192.4 2.8 gather_fusion.7
  204.0 2.5 copy.305
  206.5 2.5 convolution_add_fusion.8
  209.2 2.7 scatter_fusion
  223.4 2.8 gather_fusion.7
  235.0 2.5 copy.305
  240.2 2.8 scatter_fusion
  242.9 42.9 %all_to_all.30 = f32[32,2,256]{2,1,0:T(2,128)S(1)} all-to-all(f32[32,2,256]{2,1,0:T(2,128)S(1)} %get-tuple-element.139), channel_id=1, replica_groups=mesh['pages'=32,'mlp'=8] {'pages'}, dimensions={0} | all-to-all | bytes 131072 | tf_op jit(solution)/shard_map/all_to_all | solution.py:193
  285.8 5.0 all-to-all-start
  290.9 5.6 copy.191
  297.2 6.9 all-to-all-start.1
  305.8 52.4 %all-to-all-done.1 = f32[32,256,128]{1,2,0:T(8,128)} async-done(((f32[32,256,128]{1,2,0:T(8,128)}), f32[32,256,128]{1,2,0:T(8,128)}, u32[]{:S(2)}, u32[]{:S(2)}) %all-to-all-start.1) | async-done | bytes 4194336 | tf_op jit(solution)/shard_map/all_to_all | solution.py:191
  358.2 2.6 fusion.51
  364.0 31.6 %reduce-scatter.5.cloned.1.call-done = f32[256,128]{1,0:T(8,128)} async-done(((f32[256,1024]{1,0:T(8,128)}), f32[256,128]{1,0:T(8,128)}) %reduce-scatter.5.cloned.1.call-update) | async-done | bytes 131088 | tf_op jit(solution)/shard_map/reduce_scatter | solution.py:208
  396.7 11.6 %all-reduce.3 = (f32[256]{0:T(256)S(1)}, f32[256]{0:T(256)S(1)}) all-reduce(f32[256]{0:T(256)S(1)} %get-tuple-element.150, f32[256]{0:T(256)S(1)} %get-tuple-element.149), channel_id=1, replica_groups=mesh['pages'=32,'mlp'=8] {'mlp'}, use_global_device_ids=true, to_apply=%region_22.23 | all-reduce | flops 512 | bytes 4096 | tf_op jit(solution)/shard_map/psum | solution.py:125
  409.4 19.1 %all_gather.20 = bf16[256,1024]{1,0:T(8,128)(2,1)S(1)} all-gather(bf16[256,128]{1,0:T(8,128)(2,1)S(1)} %add_convert_fusion.3), channel_id=1, replica_groups=mesh['pages'=32,'mlp'=8] {'mlp'}, dimensions={1}, use_global_device_ids=true | all-gather | bytes 589824 | tf_op jit(solution)/shard_map/all_gather | solution.py:211
  428.6 2.9 fusion.89
  433.1 45.2 %reduce-scatter.7.cloned.1.call-done = f32[256,128]{1,0:T(8,128)} async-done(((f32[256,1024]{1,0:T(8,128)}), f32[256,128]{1,0:T(8,128)}) %reduce-scatter.7.cloned.1.call-update) | async-done | bytes 131088 | tf_op jit(solution)/shard_map/reduce_scatter | solution.py:216
  479.3 11.6 %all-reduce.2 = (f32[256]{0:T(256)S(1)}, f32[256]{0:T(256)S(1)}) all-reduce(f32[256]{0:T(256)S(1)} %get-tuple-element.148, f32[256]{0:T(256)S(1)} %get-tuple-element.147), channel_id=1, replica_groups=mesh['pages'=32,'mlp'=8] {'mlp'}, use_global_device_ids=true, to_apply=%region_27.28 | all-reduce | flops 512 | bytes 4096 | tf_op jit(solution)/shard_map/psum | solution.py:125
  492.0 19.0 %all_gather.21 = bf16[256,1024]{1,0:T(8,128)(2,1)S(1)} all-gather(bf16[256,128]{1,0:T(8,128)(2,1)S(1)} %fusion.155), channel_id=1, replica_groups=mesh['pages'=32,'mlp'=8] {'mlp'}, dimensions={1}, use_global_device_ids=true | all-gather | bytes 589824 | tf_op jit(solution)/shard_map/all_gather | solution.py:133
  512.8 61.3 %all-gather.5.cloned.1.call-done = bf16[8192,128]{1,0:T(8,128)(2,1)} async-done(((bf16[256,128]{1,0:T(8,128)(2,1)}), bf16[8192,128]{1,0:T(8,128)(2,1)}) %all-gather.5.cloned.1.call-update) | async-done | bytes 2097168 | tf_op jit(solution)/shard_map/all_gather | solution.py:184
  577.2 155.2 %while.29 = (s32[]{:T(128)}, f32[32,256,128]{2,1,0:T(8,128)}, f32[32,2,256]{2,1,0:T(2,128)}, f32[32,2,256]{2,1,0:T(2,128)S(1)}, s32[]{:T(128)}, /*index=5*/s32[6...) while((s32[]{:T(128)}, f32[32,256,128]{2,1,0:T(8,128)}, ...), condition=%wide.region_36.37_spmd, body=%wide.region_29.36_spmd.sunk | while | flops 166442464 | bytes 29996440 | solution.py:92
  588.7 2.8 gather_fusion.16
  600.3 2.5 copy.324
  605.5 2.8 scatter_fusion.3
  619.7 2.8 gather_fusion.16
  631.3 2.5 copy.324
  636.5 2.8 scatter_fusion.3
  650.8 2.8 gather_fusion.16
  662.4 2.5 copy.324
  667.6 2.8 scatter_fusion.3
  681.9 2.8 gather_fusion.16
  693.5 2.5 copy.324
  698.7 2.7 scatter_fusion.3
  712.9 2.8 gather_fusion.16
  724.5 2.5 copy.324
  729.7 2.8 scatter_fusion.3
  732.4 42.9 %all_to_all.31 = f32[32,2,256]{2,1,0:T(2,128)S(1)} all-to-all(f32[32,2,256]{2,1,0:T(2,128)S(1)} %get-tuple-element.142), channel_id=1, replica_groups=mesh['pages'=32,'mlp'=8] {'pages'}, dimensions={0} | all-to-all | bytes 131072 | tf_op jit(solution)/shard_map/all_to_all | solution.py:193
  775.3 5.0 all-to-all-start.3
  780.4 5.6 copy.193
  786.7 6.9 all-to-all-start.4
  795.3 52.4 %all-to-all-done.4 = f32[32,256,128]{1,2,0:T(8,128)} async-done(((f32[32,256,128]{1,2,0:T(8,128)}), f32[32,256,128]{1,2,0:T(8,128)}, u32[]{:S(2)}, u32[]{:S(2)}) %all-to-all-start.4) | async-done | bytes 4194336 | tf_op jit(solution)/shard_map/all_to_all | solution.py:191
  847.7 2.6 fusion.50
  852.2 32.5 %reduce-scatter.9.cloned.1.call-done = f32[256,128]{1,0:T(8,128)} async-done(((f32[256,1024]{1,0:T(8,128)}), f32[256,128]{1,0:T(8,128)}) %reduce-scatter.9.cloned.1.call-update) | async-done | bytes 131088 | tf_op jit(solution)/shard_map/reduce_scatter | solution.py:208
  885.7 12.1 %all-reduce.1 = (f32[256]{0:T(256)S(1)}, f32[256]{0:T(256)S(1)}) all-reduce(f32[256]{0:T(256)S(1)} %get-tuple-element.146, f32[256]{0:T(256)S(1)} %get-tuple-element.145), channel_id=1, replica_groups=mesh['pages'=32,'mlp'=8] {'mlp'}, use_global_device_ids=true, to_apply=%region_45.46 | all-reduce | flops 512 | bytes 4096 | tf_op jit(solution)/shard_map/psum | solution.py:125
  898.9 19.0 %all_gather.23 = bf16[256,1024]{1,0:T(8,128)(2,1)S(1)} all-gather(bf16[256,128]{1,0:T(8,128)(2,1)S(1)} %add_convert_fusion.1), channel_id=1, replica_groups=mesh['pages'=32,'mlp'=8] {'mlp'}, dimensions={1}, use_global_device_ids=true | all-gather | bytes 589824 | tf_op jit(solution)/shard_map/all_gather | solution.py:211
  917.9 4.1 fusion.87
  922.0 46.2 %reduce-scatter.11.cloned.1.call-done = f32[256,128]{1,0:T(8,128)} async-done(((f32[256,1024]{1,0:T(8,128)}), f32[256,128]{1,0:T(8,128)}) %reduce-scatter.11.cloned.1.call-update) | async-done | bytes 131088 | tf_op jit(solution)/shard_map/reduce_scatter | solution.py:216
  969.3 12.1 %all-reduce = (f32[256]{0:T(256)S(1)}, f32[256]{0:T(256)S(1)}) all-reduce(f32[256]{0:T(256)S(1)} %get-tuple-element.144, f32[256]{0:T(256)S(1)} %get-tuple-element.143), channel_id=1, replica_groups=mesh['pages'=32,'mlp'=8] {'mlp'}, use_global_device_ids=true, to_apply=%region_50.51 | all-reduce | flops 512 | bytes 4096 | tf_op jit(solution)/shard_map/psum | solution.py:125
  (449 shorter events, 253.0 us)
Async XLA Ops:
  6.5 422.0 %copy-start = (bf16[512,1024]{1,0:T(8,128)(2,1)S(1)}, bf16[512,1024]{1,0:T(8,128)(2,1)}, u32[]{:S(2)}) copy-start(bf16[512,1024]{1,0:T(8,128)(2,1)} %param.28) | copy-start | bytes 3145732
  6.5 78.1 %all-gather.3.cloned.1.call-start = ((), (), s32[]{:S(2)}) async-start(), calls=%async_computation.10 | async-start | bytes 2162688 | tf_op jit(solution)/shard_map/all_gather | solution.py:184
  30.1 0.8 copy-start.2
  85.3 2.4 copy-start.1
  285.8 11.4 %all-to-all-start = ((f32[32,2,256]{2,1,0:T(2,128)}), f32[32,2,256]{2,1,0:T(2,128)S(1)}, u32[]{:S(2)}, u32[]{:S(2)}) async-start(f32[32,2,256]{2,1,0:T(2,128)} %get-tuple-element.137), calls=%async_computation | async-start | bytes 131072 | tf_op jit(solution)/shard_map/all_to_all | solution.py:192
  296.5 7.8 copy-start.3
  296.5 7.8 copy-start.7
  296.5 8.1 copy-start.9
  297.2 61.0 %all-to-all-start.1 = ((f32[32,256,128]{1,2,0:T(8,128)}), f32[32,256,128]{1,2,0:T(8,128)}, u32[]{:S(2)}, u32[]{:S(2)}) async-start(f32[32,256,128]{1,2,0:T(8,128)} %copy.191), calls=%async_computation.1 | async-start | bytes 8388608 | tf_op jit(solution)/shard_map/all_to_all | solution.py:191
  304.2 1.1 copy-start.11
  304.2 91.5 %reduce-scatter.5.cloned.1.call-start = ((), (), s32[]{:S(2)}) async-start(), calls=%async_computation.11 | async-start | bytes 1179648 | tf_op jit(solution)/shard_map/reduce_scatter | solution.py:208
  358.2 2.9 copy-start.14
  360.9 34.8 %copy-start.13 = (bf16[256,128]{1,0:T(8,128)(2,1)S(1)}, bf16[256,128]{1,0:T(8,128)(2,1)}, u32[]{:S(2)}) copy-start(bf16[256,128]{1,0:T(8,128)(2,1)} %param.21) | copy-start | bytes 196612
  361.1 67.5 %copy-start.17 = (bf16[1024,512]{1,0:T(8,128)(2,1)S(1)}, bf16[1024,512]{1,0:T(8,128)(2,1)}, u32[]{:S(2)}) copy-start(bf16[1024,512]{1,0:T(8,128)(2,1)} %param.27) | copy-start | bytes 3145732
  362.4 115.8 %reduce-scatter.7.cloned.1.call-start = ((), (), s32[]{:S(2)}) async-start(), calls=%async_computation.12 | async-start | bytes 1179648 | tf_op jit(solution)/shard_map/reduce_scatter | solution.py:216
  428.6 4.5 copy-start.16
  431.5 80.4 %copy-start.6 = (bf16[1024,128]{1,0:T(8,128)(2,1)S(1)}, bf16[1024,128]{1,0:T(8,128)(2,1)}, u32[]{:S(2)}) copy-start(bf16[1024,128]{1,0:T(8,128)(2,1)} %param.25) | copy-start | bytes 786436
  431.5 142.6 %all-gather.5.cloned.1.call-start = ((), (), s32[]{:S(2)}) async-start(), calls=%async_computation.13 | async-start | bytes 2162688 | tf_op jit(solution)/shard_map/all_gather | solution.py:184
  511.0 0.8 copy-start.4
  775.3 11.4 %all-to-all-start.3 = ((f32[32,2,256]{2,1,0:T(2,128)}), f32[32,2,256]{2,1,0:T(2,128)S(1)}, u32[]{:S(2)}, u32[]{:S(2)}) async-start(f32[32,2,256]{2,1,0:T(2,128)} %get-tuple-element.140), calls=%async_computation.5 | async-start | bytes 131072 | tf_op jit(solution)/shard_map/all_to_all | solution.py:192
  786.0 7.8 copy-start.5
  786.0 7.8 copy-start.8
  786.0 8.1 copy-start.10
  786.7 61.0 %all-to-all-start.4 = ((f32[32,256,128]{1,2,0:T(8,128)}), f32[32,256,128]{1,2,0:T(8,128)}, u32[]{:S(2)}, u32[]{:S(2)}) async-start(f32[32,256,128]{1,2,0:T(8,128)} %copy.193), calls=%async_computation.6 | async-start | bytes 8388608 | tf_op jit(solution)/shard_map/all_to_all | solution.py:191
  793.7 1.1 copy-start.12
  793.7 91.0 %reduce-scatter.9.cloned.1.call-start = ((), (), s32[]{:S(2)}) async-start(), calls=%async_computation.14 | async-start | bytes 1179648 | tf_op jit(solution)/shard_map/reduce_scatter | solution.py:208
  847.7 2.9 copy-start.15
  851.9 116.4 %reduce-scatter.11.cloned.1.call-start = ((), (), s32[]{:S(2)}) async-start(), calls=%async_computation.15 | async-start | bytes 1179648 | tf_op jit(solution)/shard_map/reduce_scatter | solution.py:216
Sparse Core Ops, SparseCore 0:
  32.9 51.6 all-gather.2
  362.6 33.0 reduce-scatter.4
  431.6 46.6 reduce-scatter.6
  512.9 61.1 all-gather.4
  852.0 32.6 reduce-scatter.8
  922.1 46.0 reduce-scatter.10
where the time goes:
time: 1000 us; the launch traced here: 990 us
  waiting for transfers between devices  371 us (37%)
  local copies, waits for them, and re-layouts  271 us (27%)
  blocking collectives  214 us (21%)
  matrix products  65.5 us (7%)
  other arithmetic  28.8 us (3%)
  starting transfers between devices  24.4 us (2%)
  between operations  14.5 us (1%)
    all_gather x2, waiting for transfers between devices, per_device(): lax.all_gather(global_rows, 'pages', axis=0, tiled=True)  108 us
    all_to_all x2, waiting for transfers between devices, per_device(): lax.all_to_all(gathered[0], 'pages', split_axis=0, concat_axis=0, tiled=T...  105 us
    reduce_scatter x2, waiting for transfers between devices, per_device(): lax.psum_scatter(jnp.dot(active, w_down, preferred_element_type=jnp.float...  91.4 us
    all_to_all x2, blocking collectives, per_device(): lax.all_to_all(gathered[2], 'pages', split_axis=0, concat_axis=0, tiled=T...  85.8 us
    reduce_scatter x2, waiting for transfers between devices, per_device(): lax.psum_scatter(attn_term, 'mlp', scatter_dimension=1, tiled=True)  64.2 us
    psum x4, blocking collectives, norm_shares(): lax.psum((jnp.sum(totals, axis=1), jnp.sum(totals * totals, axis=1)), 'mlp')  47.4 us
    all_gather x2, blocking collectives, gather_features(): return lax.all_gather(shares, 'mlp', axis=1, tiled=True)  42.5 us
    all_gather x2, blocking collectives, per_device(): lax.all_gather(hidden_own, 'mlp', axis=1, tiled=True)  38.2 us
  transfers between devices with their start and end apart: 10, of which 10 were waited for; matrix products, arithmetic and copies ran while one was open for 2% of the time, Pallas kernels for 0%

commit v1 on v0

v1 whole, which is shorter than its diff:
```python
import functools

import jax
import jax.numpy as jnp
from jax import lax
from jax.experimental import pallas as pl
from jax.experimental.pallas import tpu as pltpu
from jax.sharding import PartitionSpec as P

HD = 64
BLK = 256
PAGE = 128
EPS = 1e-05
NEG = -1e30
CAP = 2
KEY_BLOCK = 1024
F32 = jnp.float32
BF16 = jnp.bfloat16
VMEM = pl.BlockSpec(memory_space=pltpu.VMEM)
ANY = pl.BlockSpec(memory_space=pl.ANY)
SMEM = pl.BlockSpec(memory_space=pltpu.SMEM)


def routing(page_table, me, holders, slots, hold):
    requests, pages = page_table.shape
    i32 = jnp.int32
    holder_of = jnp.where(page_table >= 0, page_table // slots, -1)
    ids = jnp.arange(holders, dtype=i32)
    page_ids = jnp.arange(pages, dtype=i32)
    on = holder_of[:, None, :] == ids[None, :, None]
    first = jnp.min(jnp.where(on, page_ids[None, None, :], pages), axis=2)
    count = jnp.sum(on.astype(i32), axis=2)
    rank = jnp.sum((first[:, None, :] < first[:, :, None]).astype(i32), axis=2)
    groups = holders // hold
    request_ids = jnp.arange(requests, dtype=i32)
    earlier = request_ids[None, :] < request_ids[:, None]

    def before(sent):
        return jnp.sum((earlier[:, :, None] & sent[None, :, :]).astype(i32), axis=1)

    my_rank = lax.dynamic_slice_in_dim(rank, me, 1, 1)
    my_count = lax.dynamic_slice_in_dim(count, me, 1, 1)
    to = (my_rank % groups == ids[None, :] // hold) & (my_count > ids[None, :] % hold)
    to_turn = before(to)
    mine = holder_of == me
    nth = jnp.sum(
        ((page_ids[None, :, None] > page_ids[None, None, :]) & mine[:, None, :]).astype(i32), axis=2
    )
    local = page_table % slots
    hit = mine[:, None, :] & (nth[:, None, :] == (ids % hold)[None, :, None])
    source = jnp.sum(jnp.where(hit, local[:, None, :], 0), axis=2)

    def send_table(turn):
        want = turn * CAP + jnp.arange(CAP, dtype=i32)
        chosen = to[:, :, None] & (to_turn[:, :, None] == want[None, None, :])
        return jnp.sum(jnp.where(chosen, source[:, :, None], 0), axis=0).reshape(-1)

    places = pages // holders
    came = (rank % groups == me // hold) & (count > me % hold)
    came_turn = before(came)

    def pass_table(turn):
        place = rank // groups
        chosen = (
            came[:, :, None]
            & (place[:, :, None] == jnp.arange(places, dtype=i32)[None, None, :])
            & (came_turn // CAP == turn)[:, :, None]
        )
        origin = ids[None, :] * CAP + came_turn % CAP + 1
        return (jnp.sum(jnp.where(chosen, origin[:, :, None], 0), axis=1) - 1).reshape(-1)

    all_to = (rank[:, :, None] % groups == ids[None, None, :] // hold) & (
        count[:, :, None] > ids[None, None, :] % hold
    )
    rounds = (jnp.max(jnp.sum(all_to.astype(i32), axis=0)) + CAP - 1) // CAP

    own_holder = lax.dynamic_slice_in_dim(holder_of, me, 1, 0)[0]
    own_rank = lax.dynamic_slice_in_dim(rank, me, 1, 0)[0]
    page_rank = jnp.sum(
        jnp.where(own_holder[:, None] == ids[None, :], own_rank[None, :], 0), axis=1
    )
    page_nth = jnp.sum(
        (
            (page_ids[None, :] < page_ids[:, None])
            & (own_holder[None, :] == own_holder[:, None])
        ).astype(i32),
        axis=1,
    )
    unit = page_rank * hold + page_nth
    found = jnp.where(own_holder >= 0, (unit % holders) * places + unit // holders, 0)
    return send_table, pass_table, rounds, found


def pack_kernel(table, keys, values, packed, sem):
    total = packed.shape[0]

    def start(i, carry):
        slot = table[i]
        pltpu.make_async_copy(keys.at[slot], packed.at[i, 0], sem).start()
        pltpu.make_async_copy(values.at[slot], packed.at[i, 1], sem).start()
        return carry

    lax.fori_loop(0, total, start, 0)
    pltpu.make_async_copy(packed, packed, sem).wait()


def pack_pages(table, keys, values):
    shape = (table.shape[0], 2) + keys.shape[1:]
    return pl.pallas_call(
        pack_kernel,
        out_shape=jax.ShapeDtypeStruct(shape, BF16),
        in_specs=[SMEM, ANY, ANY],
        out_specs=ANY,
        scratch_shapes=[pltpu.SemaphoreType.DMA],
        name="pack_pages",
    )(table, keys, values)


def repack_kernel(table, got, packed, sem):
    total = packed.shape[0]

    def start(i, carry):
        pltpu.make_async_copy(got.at[jnp.maximum(table[i], 0)], packed.at[i], sem).start()
        return carry

    lax.fori_loop(0, total, start, 0)
    pltpu.make_async_copy(packed, packed, sem).wait()


def repack_pages(table, got):
    return pl.pallas_call(
        repack_kernel,
        out_shape=jax.ShapeDtypeStruct(got.shape, BF16),
        in_specs=[SMEM, ANY],
        out_specs=ANY,
        scratch_shapes=[pltpu.SemaphoreType.DMA],
        name="repack_pages",
    )(table, got)


def exchange(pages):
    holders = lax.axis_size("pages")
    shape = pages.shape
    sent = lax.all_to_all(
        pages.reshape((holders, shape[0] // holders) + shape[1:]), "pages", 0, 0, tiled=True
    )
    return sent.reshape(shape)


def pages_to_owners(page_table, keys, values):
    holders = lax.axis_size("pages")
    me = lax.axis_index("pages")
    hold = 8
    send_table, pass_table, rounds, found = routing(page_table, me, holders, keys.shape[0], hold)
    first = exchange(pack_pages(send_table(0), keys, values))
    middle = repack_pages(pass_table(0), first)

    def further(turn, middle):
        got = exchange(pack_pages(send_table(turn), keys, values))
        table = pass_table(turn)
        return jnp.where((table >= 0)[:, None, None, None], repack_pages(table, got), middle)

    middle = lax.fori_loop(1, rounds, further, middle)
    return exchange(middle), found


def two_heads(rows):
    lane = lax.broadcasted_iota(jnp.int32, rows.shape, 1)
    low = jnp.where(lane < HD, rows, 0.0)
    high = jnp.where(lane < HD, 0.0, rows)
    return jnp.concatenate([low, high], axis=0).astype(BF16)


def attention_kernel(
    found, length, x_ref, wq, wk, wv, wg, pages, out, x_all, key_buf, value_buf, acc, peak, ksem, vsem
):
    per_block = KEY_BLOCK // PAGE
    shards = x_ref.shape[0]
    width = x_ref.shape[2]
    limit = length[0]
    blocks = (limit + KEY_BLOCK - 1) // KEY_BLOCK

    def fetch(block, carry):
        for i in range(per_block):
            page = block * per_block + i
            place = found[page]
            rows = pl.ds(pl.multiple_of(page * PAGE, PAGE), PAGE)
            pltpu.make_async_copy(pages.at[place, 0], key_buf.at[rows], ksem.at[block]).start()
            pltpu.make_async_copy(pages.at[place, 1], value_buf.at[rows], vsem.at[block]).start()
        return carry

    lax.fori_loop(0, blocks, fetch, 0)
    for i in range(shards):
        x_all[:, i * width : (i + 1) * width] = x_ref[i]
    x = x_all[...]

    def project(matrix):
        return jnp.dot(x, matrix[...], preferred_element_type=F32).astype(BF16)

    scale = HD ** (-0.5)
    queries = two_heads(project(wq).astype(F32) * scale)
    global_rows = two_heads(project(wg).astype(F32) * scale)
    key_rows = project(wk)
    value_rows = project(wv)

    def scores_of(left, keys):
        return lax.dot_general(left, keys, (((1,), (1,)), ((), ())), preferred_element_type=F32)

    def weigh(weights, values):
        ones = jnp.ones(values.shape, BF16)
        return jnp.dot(
            weights, jnp.concatenate([values, ones], axis=1), preferred_element_type=F32
        )

    scores = scores_of(queries, key_rows)
    top = jnp.max(scores, axis=1, keepdims=True)
    weights = jnp.exp(scores - top).astype(BF16)
    acc[...] = weigh(weights, value_rows)
    peak[...] = jnp.broadcast_to(top, peak.shape)

    def step(block, masked):
        rows = pl.ds(pl.multiple_of(block * KEY_BLOCK, KEY_BLOCK), KEY_BLOCK)
        pltpu.make_async_copy(key_buf.at[rows], key_buf.at[rows], ksem.at[block]).wait()
        pltpu.make_async_copy(value_buf.at[rows], value_buf.at[rows], vsem.at[block]).wait()
        scores = scores_of(global_rows, key_buf[rows, :])
        if masked:
            position = block * KEY_BLOCK + lax.broadcasted_iota(jnp.int32, scores.shape, 1)
            scores = jnp.where(position < limit, scores, NEG)
        old = peak[:, :1]
        new = jnp.maximum(old, jnp.max(scores, axis=1, keepdims=True))
        weights = jnp.exp(scores - new).astype(BF16)
        keep = jnp.exp(old - new)
        acc[...] = acc[...] * keep + weigh(weights, value_buf[rows, :])
        peak[...] = jnp.broadcast_to(new, peak.shape)

    def whole(block, carry):
        step(block, False)
        return carry

    lax.fori_loop(0, blocks - 1, whole, 0)
    step(blocks - 1, True)
    rows = x_ref.shape[1]
    total = acc[...]
    ratio = total[:, :width] / total[:, width:]
    lane = lax.broadcasted_iota(jnp.int32, (rows, width), 1)
    result = jnp.where(lane < HD, ratio[:rows], ratio[rows:]).astype(BF16)
    for i in range(shards):
        out[i] = result


def attend(found, length, x_parts, wq, wk, wv, wg, pages):
    shards, rows, width = x_parts.shape
    longest = found.shape[0] * PAGE
    return pl.pallas_call(
        attention_kernel,
        out_shape=jax.ShapeDtypeStruct(x_parts.shape, BF16),
        in_specs=[SMEM, SMEM, VMEM, VMEM, VMEM, VMEM, VMEM, ANY],
        out_specs=VMEM,
        scratch_shapes=[
            pltpu.VMEM((rows, shards * width), BF16),
            pltpu.VMEM((longest, width), BF16),
            pltpu.VMEM((longest, width), BF16),
            pltpu.VMEM((2 * rows, 2 * width), F32),
            pltpu.VMEM((2 * rows, 128), F32),
            pltpu.SemaphoreType.DMA((longest // KEY_BLOCK,)),
            pltpu.SemaphoreType.DMA((longest // KEY_BLOCK,)),
        ],
        compiler_params=pltpu.CompilerParams(vmem_limit_bytes=48 << 20),
        name="attention",
    )(found, length, x_parts, wq, wk, wv, wg, pages)


def normalize(total, gain, bias, width):
    mean = jnp.sum(total, axis=1, keepdims=True) * (1.0 / width)
    square = jnp.sum(total * total, axis=1, keepdims=True) * (1.0 / width)
    inverse = lax.rsqrt(square - mean * mean + EPS)
    return ((total - mean) * inverse * gain + bias).astype(BF16)


def ffn_kernel(
    att, x_ref, accept, w_out, up_a, up_b, down_a, down_b, g1, b1, g2, b2, out, wide, hidden, acc
):
    step = pl.program_id(0)
    shards, rows, width = x_ref.shape
    full = shards * width

    @pl.when(step == 0)
    def _():
        for i in range(shards):
            wide[:, i * width : (i + 1) * width] = att[i]
        total = jnp.dot(wide[...], w_out[...], preferred_element_type=F32)
        for i in range(shards):
            wide[:, i * width : (i + 1) * width] = x_ref[i]
        total = total + wide[...].astype(F32)
        hidden[...] = normalize(total, g1[...], b1[...], full)
        acc[...] = hidden[...].astype(F32)

    h = hidden[...]
    for up, down in ((up_a, down_a), (up_b, down_b)):
        raised = jnp.dot(h, up[0], preferred_element_type=F32)
        active = (0.5 * raised * (1.0 + lax.erf(raised * (0.5**0.5)))).astype(BF16)
        acc[...] += jnp.dot(active, down[0], preferred_element_type=F32)

    @pl.when(step == pl.num_programs(0) - 1)
    def _():
        result = normalize(acc[...], g2[...], b2[...], full)
        chosen = accept[...] != 0
        for i in range(shards):
            out[i] = jnp.where(chosen, result[:, i * width : (i + 1) * width], x_ref[i])


def feed_forward(att, x_parts, accept, w_out, up, down, g1, b1, g2, b2):
    shards, rows, width = x_parts.shape
    full = shards * width

    def fixed(shape):
        return pl.BlockSpec(shape, lambda i: (0,) * len(shape), pipeline_mode=pl.Buffered(1))

    def part(array):
        return pl.BlockSpec((1,) + array.shape[1:], lambda i: (i, 0, 0))

    return pl.pallas_call(
        ffn_kernel,
        grid=(up[0].shape[0],),
        out_shape=jax.ShapeDtypeStruct(x_parts.shape, BF16),
        in_specs=[
            fixed(x_parts.shape),
            fixed(x_parts.shape),
            fixed((rows, 1)),
            fixed(w_out.shape),
            part(up[0]),
            part(up[1]),
            part(down[0]),
            part(down[1]),
        ]
        + [fixed((1, full))] * 4,
        out_specs=pl.BlockSpec(x_parts.shape, lambda i: (0, 0, 0)),
        scratch_shapes=[
            pltpu.VMEM((rows, full), BF16),
            pltpu.VMEM((rows, full), BF16),
            pltpu.VMEM((rows, full), F32),
        ],
        compiler_params=pltpu.CompilerParams(
            dimension_semantics=("arbitrary",), vmem_limit_bytes=48 << 20
        ),
        name="feed_forward",
    )(att, x_parts, accept, w_out, up[0], up[1], down[0], down[1], g1, b1, g2, b2)


def to_all(copies):
    return lax.all_to_all(copies, "mlp", 0, 0, tiled=True)


def core_pair():
    return [(i, i ^ 1) for i in range(lax.axis_size("pages"))]


def per_device(
    embeddings,
    w_query,
    w_key,
    w_value,
    w_global_query,
    w_out,
    w_up,
    w_down,
    norm1_gain,
    norm1_bias,
    norm2_gain,
    norm2_bias,
    cache_keys,
    cache_values,
    lengths,
    page_table,
    accept,
):
    shards = lax.axis_size("mlp")
    me = lax.axis_index("pages")
    shard = lax.axis_index("mlp")
    rows, width = embeddings.shape
    pages, found = pages_to_owners(page_table, cache_keys, cache_values)
    length = lax.dynamic_slice_in_dim(lengths, me, 1, 0)

    core = me % 2
    half = w_up.shape[1] // 2
    up_half = lax.dynamic_slice_in_dim(w_up, core * half, half, 1)
    down_half = lax.dynamic_slice_in_dim(w_down, core * half, half, 0)
    w_out_all = lax.all_gather(w_out, "mlp", axis=0, tiled=True)
    up_mine = lax.all_gather(up_half, "mlp", axis=0)
    down_mine = lax.all_gather(down_half, "mlp", axis=0)
    up_other = lax.ppermute(up_mine, "pages", core_pair())
    down_other = lax.ppermute(down_mine, "pages", core_pair())
    norms = [v.reshape(1, -1) for v in (norm1_gain, norm1_bias, norm2_gain, norm2_bias)]

    x_parts = to_all(jnp.broadcast_to(embeddings[None], (shards, rows, width)))
    for pass_index in range(2):
        attention = attend(
            found, length, x_parts, w_query, w_key, w_value, w_global_query, pages
        )
        x_parts = feed_forward(
            to_all(attention),
            x_parts,
            accept[pass_index].reshape(rows, 1),
            w_out_all,
            (up_mine, up_other),
            (down_mine, down_other),
            *norms,
        )
    return lax.dynamic_index_in_dim(x_parts, shard, 0, keepdims=False)


def solution(mesh):
    return jax.shard_map(
        per_device,
        mesh=mesh,
        in_specs=(
            P("pages", "mlp"),
            P(None, "mlp"),
            P(None, "mlp"),
            P(None, "mlp"),
            P(None, "mlp"),
            P("mlp", None),
            P(None, "mlp"),
            P("mlp", None),
            P(),
            P(),
            P(),
            P(),
            P("pages", None, "mlp"),
            P("pages", None, "mlp"),
            P(),
            P(),
            P(None, "pages"),
        ),
        out_specs=P("pages", "mlp"),
        check_vma=False,
    )
```

time: 1000 us -> 517 us (0.52)
  the two profiles are of different devices: /device:TPU:9 before, /device:TPU:18 now
where the time goes in v1:
time: 517 us; the launch traced here: 511 us
  Pallas kernels  315 us (61%)
  waiting for transfers between devices  128 us (25%)
  starting transfers between devices  35.5 us (7%)
  between operations  14.2 us (3%)
  local copies, waits for them, and re-layouts  11.1 us (2%)
  other arithmetic  6.77 us (1%)
    pallas_call x1, Pallas kernels, repack_pages(): pl.pallas_call(repack_kernel, out_shape=jax.ShapeDtypeStruct(got.shape, B...  129 us
    pallas_call x1, Pallas kernels, pack_pages(): pl.pallas_call(pack_kernel, out_shape=jax.ShapeDtypeStruct(shape, BF16),...  129 us
    all_to_all x2, waiting for transfers between devices, exchange(): lax.all_to_all(pages.reshape((holders, shape[0] // holders) + shape[1:]),...  102 us
    pallas_call x2, Pallas kernels, attend(): pl.pallas_call(attention_kernel, out_shape=jax.ShapeDtypeStruct(x_parts.s...  31.1 us
    pallas_call x2, Pallas kernels, feed_forward(): pl.pallas_call(ffn_kernel, grid=(up[0].shape[0],), out_shape=jax.ShapeDty...  26.6 us
    all_to_all x3, waiting for transfers between devices, to_all(): return lax.all_to_all(copies, 'mlp', 0, 0, tiled=True)  26.2 us
    all_to_all x3, starting transfers between devices, to_all(): return lax.all_to_all(copies, 'mlp', 0, 0, tiled=True)  19.8 us
    all_to_all x2, starting transfers between devices, exchange(): lax.all_to_all(pages.reshape((holders, shape[0] // holders) + shape[1:]),...  15 us
  transfers between devices with their start and end apart: 10, of which 4 were waited for; matrix products, arithmetic and copies ran while one was open for 2% of the time, Pallas kernels for 54%

profile of v1, /device:TPU:18, one launch (start us, length us, event | category | flops | bytes accessed | tf_op | source)
XLA Modules:
  0.0 510.9 jit_solution(15745943688217621226)
XLA Ops:
  6.5 1.2 copy-done
  7.8 0.9 constant_dynamic-slice_fusion
  8.6 0.0 all-gather.8.cloned.1.call-update
  8.7 0.7 broadcast_compare_fusion.1
  9.4 1.2 convert_reduce_fusion.4
  10.6 0.8 convert_reduce_fusion.5
  11.4 0.2 fusion.22
  11.6 0.6 convert_reduce_fusion
  12.2 0.1 compare_and_fusion.1
  12.3 0.3 convert_reduce_fusion.2
  12.6 0.7 add_select_fusion.3
  13.3 0.7 select_reduce_fusion.2
  14.1 0.1 copy.25
  14.2 0.6 reshape.571.table
  14.8 128.8 %pack_pages.7 = bf16[64,2,128,128]{3,2,1,0:T(8,128)(2,1)} custom-call(s32[64]{0:T(128)} %reshape.571.table, bf16[64,128,128]{2,1,0:T(8,128)(2,1)} %keys.1, bf16[64,128,128]{2,1,0:T(8,128)(2,1)} %values.1), custom_call_target="tpu_custom_call" | custom-call | tf_op jit(solution)/shard_map/pack_pages/pallas_call | solution.py:109
  143.6 0.0 copy-start.17
  143.6 0.0 copy-start.18
  143.6 7.6 %all-to-all-start.2 = ((bf16[32,2,2,128,128]{4,3,2,1,0:T(8,128)(2,1)}), bf16[32,2,2,128,128]{4,3,2,1,0:T(8,128)(2,1)}, u32[]{:S(2)}, u32[]{:S(2)}) async-start(bf16[32,2,2,128,128]{4,3,2,1,0:T(8,128)(2,1)} %bitcast.66), calls=%async_computation.2 | async-start | bytes 8388608 | tf_op jit(solution)/shard_map/all_to_all | solution.py:144
  151.2 0.0 all-gather.10.cloned.1.call-start
  151.3 0.9 constant_dynamic-slice_fusion.1
  152.2 0.0 all-gather.10.cloned.1.call-update
  152.2 51.1 %all-to-all-done.2 = bf16[32,2,2,128,128]{4,3,2,1,0:T(8,128)(2,1)} async-done(((bf16[32,2,2,128,128]{4,3,2,1,0:T(8,128)(2,1)}), bf16[32,2,2,128,128]{4,3,2,1,0:T(8,128)(2,1)}, u32[]{:S(2)}, u32[]{:S(2)}) %all-to-all-start.2) | async-done | bytes 4194336 | tf_op jit(solution)/shard_map/all_to_all | solution.py:144
  203.3 0.9 broadcast_in_dim.167
  204.2 8.5 %all-to-all-start.1 = ((bf16[8,256,128]{2,1,0:T(8,128)(2,1)}), bf16[8,256,128]{2,1,0:T(8,128)(2,1)S(1)}, u32[]{:S(2)}, u32[]{:S(2)}) async-start(bf16[8,256,128]{2,1,0:T(8,128)(2,1)} %broadcast_in_dim.167), calls=%async_computation.1 | async-start | bytes 1048576 | tf_op jit(solution)/shard_map/all_to_all | solution.py:351
  212.7 0.3 convert_reduce_fusion.1
  213.0 0.6 reduce_max.9
  214.4 0.1 select_reduce_fusion.5
  214.5 0.1 copy.24
  214.6 0.7 sub.70.table
  215.3 128.8 %repack_pages.7 = bf16[64,2,128,128]{3,2,1,0:T(8,128)(2,1)} custom-call(s32[64]{0:T(128)} %sub.70.table, bf16[64,2,128,128]{3,2,1,0:T(8,128)(2,1)} %bitcast.3.got), custom_call_target="tpu_custom_call" | custom-call | tf_op jit(solution)/shard_map/repack_pages/pallas_call | solution.py:131
  344.2 0.0 copy-start.21
  344.2 0.0 copy-start.6
  344.2 0.0 copy-start.7
  344.2 0.0 copy-start.9
  344.2 0.0 copy-start.11
  344.2 7.4 %all-to-all-start.3 = ((bf16[32,2,2,128,128]{4,3,2,1,0:T(8,128)(2,1)}), bf16[32,2,2,128,128]{4,3,2,1,0:T(8,128)(2,1)}, u32[]{:S(2)}, u32[]{:S(2)}) async-start(bf16[32,2,2,128,128]{4,3,2,1,0:T(8,128)(2,1)} %bitcast.65), calls=%async_computation.3 | async-start | bytes 8388608 | tf_op jit(solution)/shard_map/all_to_all | solution.py:144
  351.7 0.0 copy-start.20
  351.7 0.0 copy-start.13
  351.7 0.0 copy-start.14
  351.7 0.0 all-gather.6.cloned.1.call-start
  351.8 0.0 all-gather.8.cloned.1.call-done
  351.8 0.2 collective-permute-start
  352.0 0.4 collective-permute-start.1
  352.4 0.1 all-gather.6.cloned.1.call-update
  352.5 0.6 dynamic_slice.29.length
  353.1 0.2 convert_reduce_fusion.6
  353.2 0.1 select_reduce_fusion.6
  353.4 50.4 %all-to-all-done.3 = bf16[32,2,2,128,128]{4,3,2,1,0:T(8,128)(2,1)} async-done(((bf16[32,2,2,128,128]{4,3,2,1,0:T(8,128)(2,1)}), bf16[32,2,2,128,128]{4,3,2,1,0:T(8,128)(2,1)}, u32[]{:S(2)}, u32[]{:S(2)}) %all-to-all-start.3) | async-done | bytes 4194336 | tf_op jit(solution)/shard_map/all_to_all | solution.py:144
  403.8 16.0 %attention.2 = bf16[8,256,128]{2,1,0:T(8,128)(2,1)} custom-call(s32[64]{0:T(128)S(1)} %compare_select_fusion.1.found, s32[1]{0:T(128)} %dynamic_slice.29.length, bf16[8,256,128]{2,1,0:T(8,128)(2,1)S(1)} %all-to-all-done.1.x_ref, bf16[1024,128]{1,0:T(8,128)(2,1)S(1)} %copy-done.6, bf16[1024,128]{1,0:T(8,128)(2,1)S(1)} %copy-done.7, ...), custom_call_target="tpu_custom_call" | custom-call | tf_op jit(solution)/shard_map/attention/pallas_call | solution.py:254
  419.7 7.2 %all-to-all-start.4 = ((bf16[8,256,128]{2,1,0:T(8,128)(2,1)}), bf16[8,256,128]{2,1,0:T(8,128)(2,1)S(1)}, u32[]{:S(2)}, u32[]{:S(2)}) async-start(bf16[8,256,128]{2,1,0:T(8,128)(2,1)} %attention.2), calls=%async_computation.4 | async-start | bytes 1048576 | tf_op jit(solution)/shard_map/all_to_all | solution.py:351
  427.0 0.1 copy.26.accept
  427.1 0.0 all-gather.6.cloned.1.call-done.w_out
  427.2 13.1 %all-to-all-done.4.att = bf16[8,256,128]{2,1,0:T(8,128)(2,1)S(1)} async-done(((bf16[8,256,128]{2,1,0:T(8,128)(2,1)}), bf16[8,256,128]{2,1,0:T(8,128)(2,1)S(1)}, u32[]{:S(2)}, u32[]{:S(2)}) %all-to-all-start.4) | async-done | bytes 524320 | tf_op jit(solution)/shard_map/all_to_all | solution.py:351
  440.3 1.6 copy-done.1
  441.9 13.2 %feed_forward.2.x_ref = bf16[8,256,128]{2,1,0:T(8,128)(2,1)S(1)} custom-call(bf16[8,256,128]{2,1,0:T(8,128)(2,1)S(1)} %all-to-all-done.4.att, bf16[8,256,128]{2,1,0:T(8,128)(2,1)S(1)} %all-to-all-done.1.x_ref, s32[256,1]{1,0:T(8,128)S(1)} %copy.26.accept, bf16[1024,1024]{1,0:T(8,128)(2,1)S(1)} %copy-done.1, bf16[8,1024,256]{2,1,0:T(8,128)(2,1)} %bitcast.68, ...), custom_call_target="tpu_custom_call" | custom-call | tf_op jit(solution)/shard_map/feed_forward/pallas_call | solution.py:322
  455.1 15.1 %attention.3 = bf16[8,256,128]{2,1,0:T(8,128)(2,1)S(1)} custom-call(s32[64]{0:T(128)S(1)} %compare_select_fusion.1.found, s32[1]{0:T(128)} %dynamic_slice.29.length, bf16[8,256,128]{2,1,0:T(8,128)(2,1)S(1)} %feed_forward.2.x_ref, bf16[1024,128]{1,0:T(8,128)(2,1)S(1)} %copy-done.6, bf16[1024,128]{1,0:T(8,128)(2,1)S(1)} %copy-done.8, ...), custom_call_target="tpu_custom_call" | custom-call | tf_op jit(solution)/shard_map/attention/pallas_call | solution.py:254
  470.3 0.8 copy-done.3
  471.0 0.8 copy-done.5
  471.8 4.1 all-to-all-start.5
  476.0 0.1 copy.27.accept
  476.1 13.1 %all-to-all-done.5.att = bf16[8,256,128]{2,1,0:T(8,128)(2,1)} async-done(((bf16[8,256,128]{2,1,0:T(8,128)(2,1)}), bf16[8,256,128]{2,1,0:T(8,128)(2,1)}, u32[]{:S(2)}, u32[]{:S(2)}) %all-to-all-start.5) | async-done | bytes 524320 | tf_op jit(solution)/shard_map/all_to_all | solution.py:351
  489.3 1.0 copy-done.4
  490.3 13.4 %feed_forward.3 = bf16[8,256,128]{2,1,0:T(8,128)(2,1)S(1)} custom-call(bf16[8,256,128]{2,1,0:T(8,128)(2,1)} %all-to-all-done.5.att, bf16[8,256,128]{2,1,0:T(8,128)(2,1)S(1)} %copy-done.4, s32[256,1]{1,0:T(8,128)S(1)} %copy.27.accept, bf16[1024,1024]{1,0:T(8,128)(2,1)S(1)} %copy-done.2, bf16[8,1024,256]{2,1,0:T(8,128)(2,1)} %bitcast.69, ...), custom_call_target="tpu_custom_call" | custom-call | tf_op jit(solution)/shard_map/feed_forward/pallas_call | solution.py:322
  503.7 0.6 dynamic-slice_bitcast_fusion
  (46 shorter events, 0.2 us)
Async XLA Ops:
  6.5 1.2 copy-start
  6.5 345.2 %all-gather.8.cloned.1.call-start = ((), (), s32[]{:S(2)}) async-start(), calls=%async_computation.7 | async-start | bytes 4718592 | tf_op jit(solution)/shard_map/all_gather | solution.py:389
  143.6 7.7 %copy-start.17 = (bf16[512,1024]{1,0:T(8,128)(2,1)S(1)}, bf16[512,1024]{1,0:T(8,128)(2,1)}, u32[]{:S(2)}) copy-start(bf16[512,1024]{1,0:T(8,128)(2,1)} %param.26) | copy-start | bytes 3145732
  143.6 59.7 %copy-start.18 = (bf16[256,128]{1,0:T(8,128)(2,1)S(1)}, bf16[256,128]{1,0:T(8,128)(2,1)}, u32[]{:S(2)}) copy-start(bf16[256,128]{1,0:T(8,128)(2,1)} %param.19) | copy-start | bytes 196612
  143.6 59.7 %all-to-all-start.2 = ((bf16[32,2,2,128,128]{4,3,2,1,0:T(8,128)(2,1)}), bf16[32,2,2,128,128]{4,3,2,1,0:T(8,128)(2,1)}, u32[]{:S(2)}, u32[]{:S(2)}) async-start(bf16[32,2,2,128,128]{4,3,2,1,0:T(8,128)(2,1)} %bitcast.66), calls=%async_computation.2 | async-start | bytes 8388608 | tf_op jit(solution)/shard_map/all_to_all | solution.py:144
  151.2 200.8 %all-gather.10.cloned.1.call-start = ((), (), s32[]{:S(2)}) async-start(), calls=%async_computation.8 | async-start | bytes 4718592 | tf_op jit(solution)/shard_map/all_gather | solution.py:390
  204.2 139.9 %all-to-all-start.1 = ((bf16[8,256,128]{2,1,0:T(8,128)(2,1)}), bf16[8,256,128]{2,1,0:T(8,128)(2,1)S(1)}, u32[]{:S(2)}, u32[]{:S(2)}) async-start(bf16[8,256,128]{2,1,0:T(8,128)(2,1)} %broadcast_in_dim.167), calls=%async_computation.1 | async-start | bytes 1048576 | tf_op jit(solution)/shard_map/all_to_all | solution.py:351
  344.2 8.3 %copy-start.21 = (s32[32]{0:T(128)S(1)}, s32[32]{0:T(128)}, u32[]{:S(2)}) copy-start(s32[32]{0:T(128)} %param.33) | copy-start | bytes 388
  344.2 59.6 %copy-start.6 = (bf16[1024,128]{1,0:T(8,128)(2,1)S(1)}, bf16[1024,128]{1,0:T(8,128)(2,1)}, u32[]{:S(2)}) copy-start(bf16[1024,128]{1,0:T(8,128)(2,1)} %wq.3) | copy-start | bytes 786436
  344.2 59.6 %copy-start.7 = (bf16[1024,128]{1,0:T(8,128)(2,1)S(1)}, bf16[1024,128]{1,0:T(8,128)(2,1)}, u32[]{:S(2)}) copy-start(bf16[1024,128]{1,0:T(8,128)(2,1)} %wk.3) | copy-start | bytes 786436
  344.2 59.6 %copy-start.9 = (bf16[1024,128]{1,0:T(8,128)(2,1)S(1)}, bf16[1024,128]{1,0:T(8,128)(2,1)}, u32[]{:S(2)}) copy-start(bf16[1024,128]{1,0:T(8,128)(2,1)} %wv.3) | copy-start | bytes 786436
  344.2 59.6 %copy-start.11 = (bf16[1024,128]{1,0:T(8,128)(2,1)S(1)}, bf16[1024,128]{1,0:T(8,128)(2,1)}, u32[]{:S(2)}) copy-start(bf16[1024,128]{1,0:T(8,128)(2,1)} %wg.3) | copy-start | bytes 786436
  344.2 59.5 %all-to-all-start.3 = ((bf16[32,2,2,128,128]{4,3,2,1,0:T(8,128)(2,1)}), bf16[32,2,2,128,128]{4,3,2,1,0:T(8,128)(2,1)}, u32[]{:S(2)}, u32[]{:S(2)}) async-start(bf16[32,2,2,128,128]{4,3,2,1,0:T(8,128)(2,1)} %bitcast.65), calls=%async_computation.3 | async-start | bytes 8388608 | tf_op jit(solution)/shard_map/all_to_all | solution.py:144
  351.7 75.3 %copy-start.20 = (s32[2,256]{1,0:T(2,128)S(1)}, s32[2,256]{1,0:T(2,128)}, u32[]{:S(2)}) copy-start(s32[2,256]{1,0:T(2,128)} %param.35) | copy-start | bytes 6148
  351.7 88.6 %copy-start.13 = (f32[1024]{0:T(1024)S(1)}, f32[1024]{0:T(1024)}, u32[]{:S(2)}) copy-start(f32[1024]{0:T(1024)} %param.27) | copy-start | bytes 12292
  351.7 88.6 %copy-start.14 = (f32[1024]{0:T(1024)S(1)}, f32[1024]{0:T(1024)}, u32[]{:S(2)}) copy-start(f32[1024]{0:T(1024)} %param.28) | copy-start | bytes 12292
  351.7 88.6 %copy-start.15 = (f32[1024]{0:T(1024)S(1)}, f32[1024]{0:T(1024)}, u32[]{:S(2)}) copy-start(f32[1024]{0:T(1024)} %param.29) | copy-start | bytes 12292
  351.7 88.6 %copy-start.16 = (f32[1024]{0:T(1024)S(1)}, f32[1024]{0:T(1024)}, u32[]{:S(2)}) copy-start(f32[1024]{0:T(1024)} %param.30) | copy-start | bytes 12292
  351.7 75.4 %all-gather.6.cloned.1.call-start = ((), (), s32[]{:S(2)}) async-start(), calls=%async_computation.6 | async-start | bytes 2359296 | tf_op jit(solution)/shard_map/all_gather | solution.py:388
  351.8 88.5 %collective-permute-start = (bf16[8,1024,256]{2,1,0:T(8,128)(2,1)}, bf16[8,1024,256]{2,1,0:T(8,128)(2,1)}, u32[]{:S(2)}, u32[]{:S(2)}) collective-permute-start(bf16[8,1024,256]{2,1,0:T(8,128)(2,1)} %bitcast.67), channel_id=1, source_target_pairs={{0,8},{8,0},{16,24},{24,16},{32,40},{40,32},{48,56},{56,48},{64,72... | collective-permute-start | bytes 12582920 | tf_op jit(solution)/shard_map/ppermute | solution.py:391
  352.0 88.2 %collective-permute-start.1 = (bf16[8,256,1024]{2,1,0:T(8,128)(2,1)}, bf16[8,256,1024]{2,1,0:T(8,128)(2,1)}, u32[]{:S(2)}, u32[]{:S(2)}) collective-permute-start(bf16[8,256,1024]{2,1,0:T(8,128)(2,1)} %bitcast.70), channel_id=1, source_target_pairs={{0,8},{8,0},{16,24},{24,16},{32,40},{40,32},{48,56},{56,48},{64,72... | collective-permute-start | bytes 12582920 | tf_op jit(solution)/shard_map/ppermute | solution.py:392
  419.7 20.5 %all-to-all-start.4 = ((bf16[8,256,128]{2,1,0:T(8,128)(2,1)}), bf16[8,256,128]{2,1,0:T(8,128)(2,1)S(1)}, u32[]{:S(2)}, u32[]{:S(2)}) async-start(bf16[8,256,128]{2,1,0:T(8,128)(2,1)} %attention.2), calls=%async_computation.4 | async-start | bytes 1048576 | tf_op jit(solution)/shard_map/all_to_all | solution.py:351
  440.3 1.6 copy-start.1
  441.9 13.2 %copy-start.8 = (bf16[1024,128]{1,0:T(8,128)(2,1)S(1)}, bf16[1024,128]{1,0:T(8,128)(2,1)}, u32[]{:S(2)}) copy-start(bf16[1024,128]{1,0:T(8,128)(2,1)} %wk.3) | copy-start | bytes 786436
  441.9 13.2 %copy-start.10 = (bf16[1024,128]{1,0:T(8,128)(2,1)S(1)}, bf16[1024,128]{1,0:T(8,128)(2,1)}, u32[]{:S(2)}) copy-start(bf16[1024,128]{1,0:T(8,128)(2,1)} %wv.3) | copy-start | bytes 786436
  441.9 13.2 %copy-start.12 = (bf16[1024,128]{1,0:T(8,128)(2,1)S(1)}, bf16[1024,128]{1,0:T(8,128)(2,1)}, u32[]{:S(2)}) copy-start(bf16[1024,128]{1,0:T(8,128)(2,1)} %wg.3) | copy-start | bytes 786436
  455.1 34.2 %copy-start.2 = (bf16[1024,1024]{1,0:T(8,128)(2,1)S(1)}, bf16[1024,1024]{1,0:T(8,128)(2,1)}, u32[]{:S(2)}) copy-start(bf16[1024,1024]{1,0:T(8,128)(2,1)} %all-gather.6.cloned.1.call-done.w_out) | copy-start | bytes 6291460
  470.2 0.8 copy-start.3
  471.0 0.8 copy-start.5
  471.8 17.4 %all-to-all-start.5 = ((bf16[8,256,128]{2,1,0:T(8,128)(2,1)}), bf16[8,256,128]{2,1,0:T(8,128)(2,1)}, u32[]{:S(2)}, u32[]{:S(2)}) async-start(bf16[8,256,128]{2,1,0:T(8,128)(2,1)} %copy-done.5), calls=%async_computation.5 | async-start | bytes 1048576 | tf_op jit(solution)/shard_map/all_to_all | solution.py:351
  489.3 1.0 copy-start.4
Sparse Core Ops, SparseCore 0:
  9.1 150.5 all-gather.7
  161.6 63.2 all-gather.9
  354.3 42.7 all-gather.5
